TPU v7x, 128 devices: a whole 4x4x4 slice. The times are simulated.
128 devices in a mesh: blk: 16 (over x_hi, z, core), uly: 8 (over x_lo, y).
Axes of the slice: x: 4 (x_hi: 2, x_lo: 2; x = x_hi * 2 + x_lo), y: 4, z: 4, core: 2. Of those that a mesh axis runs over, the one named last changes fastest.
Arguments:
- queries: bfloat16 [32768, 4096], P(('blk', 'uly')), may hold values from -140 to 140
- keys: bfloat16 [32768, 1024], P(('blk', 'uly')), may hold values from -6 to 6
- values: bfloat16 [32768, 1024], P(('blk', 'uly')), may hold values from -6 to 6
- doc_lengths: int32 [4], replicated, may hold values from 1 to 24576, 32768 in all
- selected: int32 [32, 8], replicated, may hold values from 0 to 30, as said below
Outputs:
- attended: bfloat16 [32768, 4096], P(('blk', 'uly'))
Inputs may be any that keep to these rules, and one draw needn't show every extreme that they name: selected[b, g] <= b, and equals b only for b = 0. For every device index along blk (blocks b with equal b // 2) and every key head, the blocks it selects that lie outside its own 2 blocks lie in distinct blocks of blk, so one other index of blk supplies at most one selected block a key head to it.
All inputs are finite; a program needn't handle non-finite values.
Results may differ from a plain program's by a relative error of at most 0.004.
Values may be sent and summed in bfloat16 or wider, within the bound.
A program may use at most 128 MiB of HBM per device.

v0:
```python
import jax
import jax.numpy as jnp
from jax import lax
from jax.sharding import PartitionSpec as P

HQ = 32
KVH = 8
HD = 128
MB = 1024


def shortened(shard):

    def short(part):
        return part.astype(jnp.bfloat16) if part.dtype == jnp.float32 else part

    return jax.tree.map(short, shard)


def on_device(queries, keys, values, doc_lengths, selected):
    q_heads, k_heads, v_heads = (
        lax.all_to_all(queries, "uly", split_axis=1, concat_axis=0, tiled=True),
        lax.all_to_all(keys, "uly", split_axis=1, concat_axis=0, tiled=True),
        lax.all_to_all(values, "uly", split_axis=1, concat_axis=0, tiled=True),
    )
    shard = k_heads.shape[0]
    kv_dev = k_heads.shape[1] // HD
    per_dev = shard // MB
    group = HQ // KVH
    scale = 1.0 / HD**0.5
    blk_index = lax.axis_index("blk")
    uly_index = lax.axis_index("uly")
    ends = jnp.cumsum(doc_lengths)

    def doc_of(places):
        return jnp.sum((ends <= places[..., None]).astype(jnp.int32), axis=-1)

    column = lax.dynamic_slice_in_dim(selected, uly_index * kv_dev, kv_dev, 1)
    mine = lax.dynamic_slice_in_dim(column, blk_index * per_dev, per_dev, 0)
    offsets = jnp.arange(MB, dtype=jnp.int32)
    k_blocks = k_heads.reshape(per_dev, MB, kv_dev, HD)
    v_blocks = v_heads.reshape(per_dev, MB, kv_dev, HD)
    empty = jnp.zeros((per_dev, kv_dev, MB, HD), jnp.bfloat16)
    k_piece = lax.all_gather(k_heads, "blk", axis=0, tiled=True)
    v_piece = lax.all_gather(v_heads, "blk", axis=0, tiled=True)
    count = k_piece.shape[0]
    wanted_rows = mine[:, :, None] * MB + offsets
    inside = (wanted_rows >= 0) & (wanted_rows < count)
    index = jnp.clip(wanted_rows, 0, count - 1)
    head_rows = jnp.arange(kv_dev, dtype=jnp.int32)[None, :, None]
    k_got = k_piece.reshape(count, kv_dev, HD)[index, head_rows]
    v_got = v_piece.reshape(count, kv_dev, HD)[index, head_rows]
    chosen_k = jnp.where(inside[..., None], k_got, empty)
    chosen_v = jnp.where(inside[..., None], v_got, empty)
    doc_query = doc_of(blk_index * shard + jnp.arange(shard, dtype=jnp.int32)).reshape(per_dev, MB)
    doc_chosen = doc_of(mine[:, :, None] * MB + offsets)
    live = mine != (blk_index * per_dev + jnp.arange(per_dev, dtype=jnp.int32))[:, None]
    q_five = q_heads.reshape(per_dev, MB, kv_dev, group, HD)
    causal = offsets[:, None] >= offsets[None, :]

    def one_block(row):
        q_now = q_five[row, :, 0]
        own_k = k_blocks[row, :, 0]
        own_v = v_blocks[row, :, 0]
        doc_now = doc_query[row]
        own_scores = (
            jnp.einsum("mgd,nd->gmn", q_now, own_k, preferred_element_type=jnp.float32) * scale
        )
        sel_scores = (
            jnp.einsum("mgd,nd->gmn", q_now, chosen_k[row, 0], preferred_element_type=jnp.float32)
            * scale
        )
        own_mask = causal & (doc_now[:, None] == doc_now[None, :])
        sel_mask = (doc_now[:, None] == doc_chosen[row, 0][None, :]) & live[row, 0]
        top = jnp.maximum(
            jnp.max(jnp.where(own_mask, own_scores, -jnp.inf), axis=-1),
            jnp.max(jnp.where(sel_mask, sel_scores, -jnp.inf), axis=-1),
        )
        own_weight = jnp.where(own_mask, jnp.exp(own_scores - top[..., None]), 0.0)
        sel_weight = jnp.where(sel_mask, jnp.exp(sel_scores - top[..., None]), 0.0)
        total = jnp.sum(own_weight, axis=-1) + jnp.sum(sel_weight, axis=-1)
        acc = jnp.einsum(
            "gmn,nd->mgd",
            own_weight.astype(jnp.bfloat16),
            own_v,
            preferred_element_type=jnp.float32,
        )
        acc = acc + jnp.einsum(
            "gmn,nd->mgd",
            sel_weight.astype(jnp.bfloat16),
            chosen_v[row, 0],
            preferred_element_type=jnp.float32,
        )
        output = (acc / jnp.transpose(total)[:, :, None]).astype(jnp.bfloat16)
        results = [output.reshape(MB, group * HD)]
        return jnp.concatenate(results, axis=1)

    blocks = lax.map(one_block, jnp.arange(per_dev, dtype=jnp.int32))
    head_major = blocks.reshape(shard, kv_dev * group * HD)
    return lax.all_to_all(
        shortened(head_major), "uly", split_axis=0, concat_axis=1, tiled=True
    ).astype(head_major.dtype)


def solution(mesh):
    placed = (P(("blk", "uly"), None), P(("blk", "uly"), None), P(("blk", "uly"), None), P(), P())
    return jax.shard_map(
        on_device, mesh=mesh, in_specs=placed, out_specs=P(("blk", "uly"), None), check_vma=False
    )
```

profile of v0, /device:TPU:0, one launch (start us, length us, event | category | flops | bytes accessed | tf_op | source)
XLA Modules:
  0.0 339.3 jit_solution(10035589432104716026)
XLA Ops:
  6.5 1.3 copy.43
  7.8 15.3 %all_to_all.73 = bf16[256,8,128]{0,2,1:T(8,128)(2,1)S(1)} all-to-all(bf16[256,8,128]{0,2,1:T(8,128)(2,1)S(1)} %bitcast.166), channel_id=1, replica_groups=mesh['blk'=16,'uly'=8] {'uly'}, dimensions={1} | all-to-all | bytes 1048576 | tf_op jit(solution)/shard_map/all_to_all | solution.py:24
  24.4 11.7 %all_to_all.74 = bf16[256,8,128]{2,0,1:T(8,128)(2,1)} all-to-all(bf16[256,8,128]{2,0,1:T(8,128)(2,1)S(1)} %copy_bitcast_fusion.4), channel_id=1, replica_groups=mesh['blk'=16,'uly'=8] {'uly'}, dimensions={1} | all-to-all | bytes 1048576 | tf_op jit(solution)/shard_map/all_to_all | solution.py:23
  36.1 3.1 copy.80
  39.3 3.6 %all-to-all-start.2 = ((bf16[256,8,512]{2,0,1:T(8,128)(2,1)}), bf16[256,8,512]{2,0,1:T(8,128)(2,1)S(1)}, u32[]{:S(2)}, u32[]{:S(2)}) async-start(bf16[256,8,512]{2,0,1:T(8,128)(2,1)} %bitcast.154), calls=%async_computation.2 | async-start | bytes 4194304 | tf_op jit(solution)/shard_map/all_to_all | solution.py:22
  45.2 27.4 %all-to-all-done.2 = bf16[256,8,512]{2,0,1:T(8,128)(2,1)S(1)} async-done(((bf16[256,8,512]{2,0,1:T(8,128)(2,1)}), bf16[256,8,512]{2,0,1:T(8,128)(2,1)S(1)}, u32[]{:S(2)}, u32[]{:S(2)}) %all-to-all-start.2) | async-done | bytes 2097184 | tf_op jit(solution)/shard_map/all_to_all | solution.py:22
  72.6 2.1 reshape.225
  74.7 27.1 %all-gather.5.cloned.1.call-done = bf16[32768,128]{1,0:T(8,128)(2,1)} async-done(((bf16[2048,128]{1,0:T(8,128)(2,1)}), bf16[32768,128]{1,0:T(8,128)(2,1)}) %all-gather.5.cloned.1.call-update) | async-done | bytes 8388624 | tf_op jit(solution)/shard_map/all_gather | solution.py:45
  101.8 22.6 %gather_fusion.1 = bf16[2048,128]{1,0:T(8,128)(2,1)S(1)} fusion(bf16[32768,1,128]{2,0,1:T(8,128)(2,1)} %bitcast.157, s32[2048]{0:T(1024)S(1)} %bitcast.150), kind=kCustom, calls=%fused_computation.1 | custom fusion | bytes 1064960 | tf_op jit(solution)/shard_map/gather | solution.py:52
  124.7 50.9 %all-gather.3.cloned.1.call-done = bf16[32768,128]{1,0:T(8,128)(2,1)} async-done(((bf16[2048,128]{1,0:T(8,128)(2,1)}), bf16[32768,128]{1,0:T(8,128)(2,1)}) %all-gather.3.cloned.1.call-update) | async-done | bytes 8388624 | tf_op jit(solution)/shard_map/all_gather | solution.py:44
  175.6 22.6 %gather_fusion = bf16[2048,128]{1,0:T(8,128)(2,1)S(1)} fusion(bf16[32768,1,128]{2,0,1:T(8,128)(2,1)} %bitcast.158, s32[2048]{0:T(1024)S(1)} %bitcast.151), kind=kCustom, calls=%fused_computation | custom fusion | bytes 1064960 | tf_op jit(solution)/shard_map/gather | solution.py:51
  198.4 1.1 broadcast_select_fusion
  199.5 94.8 %while.11 = (s32[]{:T(128)}, bf16[2,1024,512]{2,1,0:T(8,128)(2,1)}, s32[2]{0:T(128)S(1)}, bf16[2,1024,1,128]{3,1,0,2:T(8,128)(2,1)S(1)}, s32[2,1024]{1,0:T(2,128...) while((s32[]{:T(128)}, bf16[2,1024,512]{2,1,0:T(8,128)(2,1)}, ...), condition=%wide.region_8.9_spmd.clone, body=%wide.region_3.8_spmd.clone.sunk | while | flops 4394049536 | bytes 123986648 | solution.py:98
  202.5 2.5 compare_and_fusion.3
  205.0 1.6 constant_dynamic-slice_fusion.11
  206.6 4.0 %fusion.59 = (f32[4,1024]{1,0:T(4,128)S(1)}, f32[1024,1024,4]{1,0,2:T(8,128)S(1)}) fusion(pred[1024,1024]{0,1:T(8,128)(4,1)S(1)} %get-tuple-element.245, bf16[1,1024,1,4,128]{4,3,1,0,2:T(4,128)(2,1)S(1)} %constant_dynamic-slice_fusion.11, bf16[2,1024,1,128]{3,1,2,0:T(8,128)(2,1)} %get-tuple-element.284, s32[]{:T(128)S(6)} %select_n.115), kind=kOutput, calls=%fused_computation.10.clone.1 | convolution fusion | flops 1086320640 | bytes 19152900 | tf_op jit(solution)/shard_map/while/body/eval_jaxpr/mgd,nd->gmn/dot_general | solution.py:67
  210.6 8.5 %fusion.58 = (f32[4,1024]{1,0:T(4,128)S(1)}, f32[1024,1024,4]{1,0,2:T(8,128)}) fusion(pred[1024,1024]{0,1:T(8,128)(4,1)S(1)} %get-tuple-element.243, bf16[1,1024,1,4,128]{4,3,1,0,2:T(4,128)(2,1)S(1)} %constant_dynamic-slice_fusion.11, bf16[2,1,1024,128]{2,3,1,0:T(8,128)(2,1)} %get-tuple-element.288, s32[]{:T(128)S(6)} %select_n.115), kind=kOutput, calls=%fused_computation.5.clone.1 | convolution fusion | flops 1086320640 | bytes 19152900 | tf_op jit(solution)/shard_map/while/body/eval_jaxpr/mgd,nd->gmn/dot_general | solution.py:70
  219.1 9.9 %fusion.61 = (f32[4,1024]{1,0:T(4,128)S(1)}, f32[4,1024]{1,0:T(4,128)S(1)}) fusion(f32[1024,1024,4]{1,0,2:T(8,128)} %get-tuple-element.244, f32[4,1024]{1,0:T(4,128)S(1)} %max.13, pred[1024,1024]{0,1:T(8,128)(4,1)S(1)} %get-tuple-element.243, f32[1024,1024,4]{1,0,2:T(8,128)S(1)} %get-tuple-element.248, pred[1024,1024]{0,1:T(8,128)(4,1)S(1)} %get-tuple-element.245), kind=kLoop, calls=%fused_computation.15.clone.1 | loop fusion | flops 33546240 | bytes 35700736 | tf_op jit(solution)/shard_map/while/body/eval_jaxpr/reduce_sum | solution.py:81
  229.1 11.0 %fusion.60 = f32[128,4,1024]{2,0,1:T(8,128)} fusion(f32[1024,1024,4]{1,0,2:T(8,128)} %get-tuple-element.244, f32[4,1024]{1,0:T(4,128)S(1)} %max.13, pred[1024,1024]{0,1:T(8,128)(4,1)S(1)} %get-tuple-element.243, bf16[2,1,1024,128]{2,3,1,0:T(8,128)(2,1)} %get-tuple-element.289, s32[]{:T(128)S(6)} %select_n.115), kind=kOutput, calls=%fused_computation.17.clone.1 | convolution fusion | flops 1090519040 | bytes 20201476 | tf_op jit(solution)/shard_map/while/body/eval_jaxpr/gmn,nd->mgd/dot_general | solution.py:88
  240.1 5.2 %fusion.62 = bf16[1024,4,128]{0,2,1:T(8,128)(2,1)S(1)} fusion(f32[128,4,1024]{2,0,1:T(8,128)} %fusion.60, f32[1024,1024,4]{1,0,2:T(8,128)S(1)} %get-tuple-element.248, f32[4,1024]{1,0:T(4,128)S(1)} %max.13, pred[1024,1024]{0,1:T(8,128)(4,1)S(1)} %get-tuple-element.245, f32[1024,4]{0,1:T(4,128)S(1)} %add_bitcast_fusion.2, ...), kind=kOutput, calls=%fused_computation.25.clone.1 | convolution fusion | flops 1092091904 | bytes 21266436 | tf_op jit(solution)/shard_map/while/body/eval_jaxpr/gmn,nd->mgd/dot_general | solution.py:82
  245.9 1.0 constant_dynamic-update-slice_fusion.2
  249.9 2.5 compare_and_fusion.3
  252.4 1.6 constant_dynamic-slice_fusion.11
  254.0 4.0 %fusion.59 = (f32[4,1024]{1,0:T(4,128)S(1)}, f32[1024,1024,4]{1,0,2:T(8,128)S(1)}) fusion(pred[1024,1024]{0,1:T(8,128)(4,1)S(1)} %get-tuple-element.245, bf16[1,1024,1,4,128]{4,3,1,0,2:T(4,128)(2,1)S(1)} %constant_dynamic-slice_fusion.11, bf16[2,1024,1,128]{3,1,2,0:T(8,128)(2,1)} %get-tuple-element.284, s32[]{:T(128)S(6)} %select_n.115), kind=kOutput, calls=%fused_computation.10.clone.1 | convolution fusion | flops 1086320640 | bytes 19152900 | tf_op jit(solution)/shard_map/while/body/eval_jaxpr/mgd,nd->gmn/dot_general | solution.py:67
  258.0 8.5 %fusion.58 = (f32[4,1024]{1,0:T(4,128)S(1)}, f32[1024,1024,4]{1,0,2:T(8,128)}) fusion(pred[1024,1024]{0,1:T(8,128)(4,1)S(1)} %get-tuple-element.243, bf16[1,1024,1,4,128]{4,3,1,0,2:T(4,128)(2,1)S(1)} %constant_dynamic-slice_fusion.11, bf16[2,1,1024,128]{2,3,1,0:T(8,128)(2,1)} %get-tuple-element.288, s32[]{:T(128)S(6)} %select_n.115), kind=kOutput, calls=%fused_computation.5.clone.1 | convolution fusion | flops 1086320640 | bytes 19152900 | tf_op jit(solution)/shard_map/while/body/eval_jaxpr/mgd,nd->gmn/dot_general | solution.py:70
  266.5 9.9 %fusion.61 = (f32[4,1024]{1,0:T(4,128)S(1)}, f32[4,1024]{1,0:T(4,128)S(1)}) fusion(f32[1024,1024,4]{1,0,2:T(8,128)} %get-tuple-element.244, f32[4,1024]{1,0:T(4,128)S(1)} %max.13, pred[1024,1024]{0,1:T(8,128)(4,1)S(1)} %get-tuple-element.243, f32[1024,1024,4]{1,0,2:T(8,128)S(1)} %get-tuple-element.248, pred[1024,1024]{0,1:T(8,128)(4,1)S(1)} %get-tuple-element.245), kind=kLoop, calls=%fused_computation.15.clone.1 | loop fusion | flops 33546240 | bytes 35700736 | tf_op jit(solution)/shard_map/while/body/eval_jaxpr/reduce_sum | solution.py:81
  276.5 11.0 %fusion.60 = f32[128,4,1024]{2,0,1:T(8,128)} fusion(f32[1024,1024,4]{1,0,2:T(8,128)} %get-tuple-element.244, f32[4,1024]{1,0:T(4,128)S(1)} %max.13, pred[1024,1024]{0,1:T(8,128)(4,1)S(1)} %get-tuple-element.243, bf16[2,1,1024,128]{2,3,1,0:T(8,128)(2,1)} %get-tuple-element.289, s32[]{:T(128)S(6)} %select_n.115), kind=kOutput, calls=%fused_computation.17.clone.1 | convolution fusion | flops 1090519040 | bytes 20201476 | tf_op jit(solution)/shard_map/while/body/eval_jaxpr/gmn,nd->mgd/dot_general | solution.py:88
  287.4 5.2 %fusion.62 = bf16[1024,4,128]{0,2,1:T(8,128)(2,1)S(1)} fusion(f32[128,4,1024]{2,0,1:T(8,128)} %fusion.60, f32[1024,1024,4]{1,0,2:T(8,128)S(1)} %get-tuple-element.248, f32[4,1024]{1,0:T(4,128)S(1)} %max.13, pred[1024,1024]{0,1:T(8,128)(4,1)S(1)} %get-tuple-element.245, f32[1024,4]{0,1:T(4,128)S(1)} %add_bitcast_fusion.2, ...), kind=kOutput, calls=%fused_computation.25.clone.1 | convolution fusion | flops 1092091904 | bytes 21266436 | tf_op jit(solution)/shard_map/while/body/eval_jaxpr/gmn,nd->mgd/dot_general | solution.py:82
  293.2 1.0 constant_dynamic-update-slice_fusion.2
  294.3 31.7 %all_to_all.75 = bf16[8,256,512]{2,1,0:T(8,128)(2,1)S(1)} all-to-all(bf16[8,256,512]{2,1,0:T(8,128)(2,1)} %bitcast.160), channel_id=1, replica_groups=mesh['blk'=16,'uly'=8] {'uly'}, dimensions={0} | all-to-all | bytes 4194304 | tf_op jit(solution)/shard_map/all_to_all | solution.py:100
  326.0 2.4 copy.56
  328.4 4.1 %copy.57 = bf16[256,4096]{1,0:T(8,128)(2,1)} copy(bf16[256,4096]{0,1:T(8,128)(2,1)} %bitcast.156) | data formatting | bytes 4194304 | tf_op jit(solution)/shard_map/all_to_all | solution.py:100
  (45 shorter events, 7.4 us)
Async XLA Ops:
  6.5 17.7 %copy-start = (bf16[256,1024]{1,0:T(8,128)(2,1)S(1)}, bf16[256,1024]{1,0:T(8,128)(2,1)}, u32[]{:S(2)}) copy-start(bf16[256,1024]{1,0:T(8,128)(2,1)} %param.8) | copy-start | bytes 1572868
  6.5 95.3 %all-gather.5.cloned.1.call-start = ((), (), s32[]{:S(2)}) async-start(), calls=%async_computation.5 | async-start | bytes 8912896 | tf_op jit(solution)/shard_map/all_gather | solution.py:45
  24.2 175.3 %copy-start.2 = (bf16[8,256,128]{2,1,0:T(8,128)(2,1)S(1)}, bf16[8,256,128]{2,1,0:T(8,128)(2,1)}, u32[]{:S(2)}) copy-start(bf16[8,256,128]{2,1,0:T(8,128)(2,1)} %copy.44) | copy-start | bytes 1572868
  24.2 151.4 %all-gather.3.cloned.1.call-start = ((), (), s32[]{:S(2)}) async-start(), calls=%async_computation.4 | async-start | bytes 8912896 | tf_op jit(solution)/shard_map/all_gather | solution.py:44
  39.3 33.4 %all-to-all-start.2 = ((bf16[256,8,512]{2,0,1:T(8,128)(2,1)}), bf16[256,8,512]{2,0,1:T(8,128)(2,1)S(1)}, u32[]{:S(2)}, u32[]{:S(2)}) async-start(bf16[256,8,512]{2,0,1:T(8,128)(2,1)} %bitcast.154), calls=%async_computation.2 | async-start | bytes 4194304 | tf_op jit(solution)/shard_map/all_to_all | solution.py:22
  294.3 38.1 %copy-start.1 = (bf16[256,1024]{1,0:T(8,128)(2,1)S(1)}, bf16[256,1024]{1,0:T(8,128)(2,1)}, u32[]{:S(2)}) copy-start(bf16[256,1024]{1,0:T(8,128)(2,1)} %param.8) | copy-start | bytes 1572868
Sparse Core Ops, SparseCore 0:
  24.3 77.4 all-gather.4
  104.3 71.2 all-gather.2
where the time goes:
time: 341 us; the launch traced here: 339 us
  waiting for transfers between devices  105 us (31%)
  local copies, waits for them, and re-layouts  69.3 us (20%)
  blocking collectives  58.8 us (17%)
  matrix products  57.4 us (17%)
  other arithmetic  27.3 us (8%)
  between operations  13.5 us (4%)
  loops' own time  3.8 us (1%)
  starting transfers between devices  3.65 us (1%)
    all_gather x1, waiting for transfers between devices, on_device(): k_piece = lax.all_gather(k_heads, 'blk', axis=0, tiled=True)  50.9 us
    all_to_all x1, blocking collectives, on_device(): lax.all_to_all(shortened(head_major), 'uly', split_axis=0, concat_axis=1,...  31.7 us
    all_to_all x1, waiting for transfers between devices, on_device(): lax.all_to_all(queries, 'uly', split_axis=1, concat_axis=0, tiled=True)  27.4 us
    all_gather x1, waiting for transfers between devices, on_device(): v_piece = lax.all_gather(v_heads, 'blk', axis=0, tiled=True)  27.1 us
    gather x2, local copies, waits for them, and re-layouts, on_device(): v_got = v_piece.reshape(count, kv_dev, HD)[index, head_rows]  22.8 us
    gather x2, local copies, waits for them, and re-layouts, on_device(): k_got = k_piece.reshape(count, kv_dev, HD)[index, head_rows]  22.8 us
    dot_general x2, matrix products, one_block(): jnp.einsum('gmn,nd->mgd', sel_weight.astype(jnp.bfloat16), chosen_v[row,...  21.9 us
    reduce_sum x2, other arithmetic, one_block(): total = jnp.sum(own_weight, axis=-1) + jnp.sum(sel_weight, axis=-1)  19.9 us
  transfers between devices with their start and end apart: 3, of which 3 were waited for; matrix products, arithmetic and copies ran while one was open for 9% of the time, Pallas kernels for 0%

commit v1 on v0

--- a/solution.py
+++ b/solution.py
@@ -7,6 +7,16 @@
 KVH = 8
 HD = 128
 MB = 1024
+
+
+def clear_signs_on(local_array, t0, shard_axis):
+    return jnp.split(
+        lax.all_gather(
+            jnp.concatenate([local_array, t0], axis=1), axis_name=shard_axis, axis=0, tiled=True
+        ),
+        [local_array.shape[1]],
+        axis=1,
+    )
 
 
 def shortened(shard):
@@ -41,8 +51,7 @@
     k_blocks = k_heads.reshape(per_dev, MB, kv_dev, HD)
     v_blocks = v_heads.reshape(per_dev, MB, kv_dev, HD)
     empty = jnp.zeros((per_dev, kv_dev, MB, HD), jnp.bfloat16)
-    k_piece = lax.all_gather(k_heads, "blk", axis=0, tiled=True)
-    v_piece = lax.all_gather(v_heads, "blk", axis=0, tiled=True)
+    k_piece, v_piece = clear_signs_on(k_heads, v_heads, "blk")
     count = k_piece.shape[0]
     wanted_rows = mine[:, :, None] * MB + offsets
     inside = (wanted_rows >= 0) & (wanted_rows < count)

time: 341 us -> 359 us (1.053)
  blocking collectives: 58.8 us -> 31.6 us
  waiting for transfers between devices: 105 us -> 130 us
  local copies, waits for them, and re-layouts: 69.3 us -> 80.7 us
  starting transfers between devices: 3.65 us -> 12.6 us
    all_to_all x2 -> x0, blocking collectives: 27.1 us -> none  [the longest x1 15.3 us: on_device(): lax.all_to_all(values, 'uly', split_axis=1, concat_axis=0, tiled=True)]
    all_to_all x0 -> x2, waiting for transfers between devices: none -> 17.1 us  [the longest x1 8.69 us: on_device(): lax.all_to_all(values, 'uly', split_axis=1, concat_axis=0, tiled=True)]
    reshape x0 -> x1, local copies, waits for them, and re-layouts: none -> 11.3 us  [on_device(): v_got = v_piece.reshape(count, kv_dev, HD)[index, head_rows]]
    all_to_all x0 -> x2, starting transfers between devices: none -> 8.97 us  [the longest x1 5.48 us: on_device(): lax.all_to_all(values, 'uly', split_axis=1, concat_axis=0, tiled=True)]
    all_to_all x1, waiting for transfers between devices: 27.4 us -> 34.2 us  [on_device(): lax.all_to_all(queries, 'uly', split_axis=1, concat_axis=0, tiled=True)]
    all_gather x2 -> x1, waiting for transfers between devices: 78 us -> 78.2 us  [clear_signs_on(): lax.all_gather(jnp.concatenate([local_array, t0], axis=1), axis_name=shar...]
  transfers between devices with their start and end apart: 3 -> 4, of which waited for: 3 -> 4; matrix products, arithmetic and copies ran while one was open for 9% -> 2% of each run, Pallas kernels for 0% -> 0%
where the time goes in v1:
time: 359 us; the launch traced here: 357 us
  waiting for transfers between devices  130 us (36%)
  local copies, waits for them, and re-layouts  80.7 us (22%)
  matrix products  55.7 us (16%)
  blocking collectives  31.6 us (9%)
  other arithmetic  29.1 us (8%)
  between operations  13.5 us (4%)
  starting transfers between devices  12.6 us (4%)
  loops' own time  4.29 us (1%)
    all_gather x1, waiting for transfers between devices, clear_signs_on(): lax.all_gather(jnp.concatenate([local_array, t0], axis=1), axis_name=shar...  78.2 us
    all_to_all x1, waiting for transfers between devices, on_device(): lax.all_to_all(queries, 'uly', split_axis=1, concat_axis=0, tiled=True)  34.2 us
    all_to_all x1, blocking collectives, on_device(): lax.all_to_all(shortened(head_major), 'uly', split_axis=0, concat_axis=1,...  31.6 us
    gather x2, local copies, waits for them, and re-layouts, on_device(): k_got = k_piece.reshape(count, kv_dev, HD)[index, head_rows]  22.8 us
    gather x2, local copies, waits for them, and re-layouts, on_device(): v_got = v_piece.reshape(count, kv_dev, HD)[index, head_rows]  22.7 us
    dot_general x2, matrix products, one_block(): jnp.einsum('gmn,nd->mgd', sel_weight.astype(jnp.bfloat16), chosen_v[row,...  22 us
    reduce_sum x2, other arithmetic, one_block(): total = jnp.sum(own_weight, axis=-1) + jnp.sum(sel_weight, axis=-1)  19.9 us
    dot_general x2, matrix products, one_block(): jnp.einsum('mgd,nd->gmn', q_now, chosen_k[row, 0], preferred_element_type...  17 us
  transfers between devices with their start and end apart: 4, of which 4 were waited for; matrix products, arithmetic and copies ran while one was open for 2% of the time, Pallas kernels for 0%

profile of v1, /device:TPU:0, one launch (start us, length us, event | category | flops | bytes accessed | tf_op | source)
XLA Modules:
  0.0 357.2 jit_solution(13733822805454754690)
XLA Ops:
  6.5 2.2 copy.43
  8.7 5.5 %all-to-all-start = ((bf16[256,8,128]{0,2,1:T(8,128)(2,1)}), bf16[256,8,128]{0,2,1:T(8,128)(2,1)S(1)}, u32[]{:S(2)}, u32[]{:S(2)}) async-start(bf16[256,8,128]{0,2,1:T(8,128)(2,1)} %bitcast.162), calls=%async_computation | async-start | bytes 1048576 | tf_op jit(solution)/shard_map/all_to_all | solution.py:34
  15.1 8.7 %all-to-all-done = bf16[256,8,128]{0,2,1:T(8,128)(2,1)S(1)} async-done(((bf16[256,8,128]{0,2,1:T(8,128)(2,1)}), bf16[256,8,128]{0,2,1:T(8,128)(2,1)S(1)}, u32[]{:S(2)}, u32[]{:S(2)}) %all-to-all-start) | async-done | bytes 524320 | tf_op jit(solution)/shard_map/all_to_all | solution.py:34
  23.8 3.5 all-to-all-start.1
  28.4 8.4 %all-to-all-done.1 = bf16[256,8,128]{2,0,1:T(8,128)(2,1)S(1)} async-done(((bf16[256,8,128]{2,0,1:T(8,128)(2,1)}), bf16[256,8,128]{2,0,1:T(8,128)(2,1)S(1)}, u32[]{:S(2)}, u32[]{:S(2)}) %all-to-all-start.1) | async-done | bytes 524320 | tf_op jit(solution)/shard_map/all_to_all | solution.py:33
  36.8 2.3 pad_maximum_fusion
  39.2 1.6 copy.80
  40.7 3.6 %all-to-all-start.2 = ((bf16[256,8,512]{2,0,1:T(8,128)(2,1)}), bf16[256,8,512]{2,0,1:T(8,128)(2,1)S(1)}, u32[]{:S(2)}, u32[]{:S(2)}) async-start(bf16[256,8,512]{2,0,1:T(8,128)(2,1)} %bitcast.156), calls=%async_computation.2 | async-start | bytes 4194304 | tf_op jit(solution)/shard_map/all_to_all | solution.py:32
  46.0 34.2 %all-to-all-done.2 = bf16[256,8,512]{2,0,1:T(8,128)(2,1)S(1)} async-done(((bf16[256,8,512]{2,0,1:T(8,128)(2,1)}), bf16[256,8,512]{2,0,1:T(8,128)(2,1)S(1)}, u32[]{:S(2)}, u32[]{:S(2)}) %all-to-all-start.2) | async-done | bytes 2097184 | tf_op jit(solution)/shard_map/all_to_all | solution.py:32
  80.2 2.0 reshape.225
  82.3 78.2 %all-gather.2.cloned.1.call-done = bf16[32768,256]{1,0:T(8,128)(2,1)} async-done(((bf16[2048,256]{1,0:T(8,128)(2,1)}), bf16[32768,256]{1,0:T(8,128)(2,1)}) %all-gather.2.cloned.1.call-update) | async-done | bytes 16777232 | tf_op jit(solution)/shard_map/all_gather | solution.py:14
  160.5 11.3 %slice_bitcast_fusion = (bf16[32768,1,128]{2,0,1:T(8,128)(2,1)}, bf16[32768,1,128]{2,0,1:T(8,128)(2,1)}) fusion(bf16[32768,256]{1,0:T(8,128)(2,1)} %all-gather.2.cloned.1.call-done), kind=kLoop, calls=%fused_computation.51 | loop fusion | bytes 33554432 | tf_op jit(solution)/shard_map/reshape | solution.py:61
  171.8 22.5 %gather_fusion = bf16[2048,128]{1,0:T(8,128)(2,1)S(1)} fusion(bf16[32768,1,128]{2,0,1:T(8,128)(2,1)} %get-tuple-element.167, s32[2048]{0:T(1024)S(1)} %bitcast.152), kind=kCustom, calls=%fused_computation | custom fusion | bytes 1064960 | tf_op jit(solution)/shard_map/gather | solution.py:60
  194.6 22.5 %gather_fusion.1 = bf16[2048,128]{1,0:T(8,128)(2,1)S(1)} fusion(bf16[32768,1,128]{2,0,1:T(8,128)(2,1)} %get-tuple-element.166, s32[2048]{0:T(1024)S(1)} %bitcast.153), kind=kCustom, calls=%fused_computation.1 | custom fusion | bytes 1064960 | tf_op jit(solution)/shard_map/gather | solution.py:61
  218.4 93.9 %while.11 = (s32[]{:T(128)}, bf16[2,1024,512]{2,1,0:T(8,128)(2,1)}, s32[2]{0:T(128)S(1)}, bf16[2,1024,1,128]{3,1,0,2:T(8,128)(2,1)}, s32[2,1024]{1,0:T(2,128)S(1...) while((s32[]{:T(128)}, bf16[2,1024,512]{2,1,0:T(8,128)(2,1)}, ...), condition=%wide.region_8.9_spmd.clone, body=%wide.region_3.8_spmd.clone.sunk | while | flops 4394049536 | bytes 123986648 | solution.py:107
  221.7 2.5 compare_and_fusion.3
  224.3 1.6 constant_dynamic-slice_fusion.11
  225.9 3.1 fusion.59
  228.9 8.5 %fusion.58 = (f32[4,1024]{1,0:T(4,128)S(1)}, f32[1024,1024,4]{1,0,2:T(8,128)}) fusion(pred[1024,1024]{0,1:T(8,128)(4,1)S(1)} %get-tuple-element.245, bf16[1,1024,1,4,128]{4,3,1,0,2:T(4,128)(2,1)S(1)} %constant_dynamic-slice_fusion.11, bf16[2,1,1024,128]{2,3,1,0:T(8,128)(2,1)} %get-tuple-element.290, s32[]{:T(128)S(6)} %select_n.115), kind=kOutput, calls=%fused_computation.5.clone.1 | convolution fusion | flops 1086320640 | bytes 19152900 | tf_op jit(solution)/shard_map/while/body/eval_jaxpr/mgd,nd->gmn/dot_general | solution.py:79
  237.5 9.9 %fusion.61 = (f32[4,1024]{1,0:T(4,128)S(1)}, f32[4,1024]{1,0:T(4,128)S(1)}) fusion(f32[1024,1024,4]{1,0,2:T(8,128)} %get-tuple-element.246, f32[4,1024]{1,0:T(4,128)S(1)} %max.13, pred[1024,1024]{0,1:T(8,128)(4,1)S(1)} %get-tuple-element.245, f32[1024,1024,4]{1,0,2:T(8,128)S(1)} %get-tuple-element.250, pred[1024,1024]{0,1:T(8,128)(4,1)S(1)} %get-tuple-element.247), kind=kLoop, calls=%fused_computation.15.clone.1 | loop fusion | flops 33546240 | bytes 35700736 | tf_op jit(solution)/shard_map/while/body/eval_jaxpr/reduce_sum | solution.py:90
  247.4 11.0 %fusion.60 = f32[128,4,1024]{2,0,1:T(8,128)} fusion(f32[1024,1024,4]{1,0,2:T(8,128)} %get-tuple-element.246, f32[4,1024]{1,0:T(4,128)S(1)} %max.13, pred[1024,1024]{0,1:T(8,128)(4,1)S(1)} %get-tuple-element.245, bf16[2,1,1024,128]{2,3,1,0:T(8,128)(2,1)} %get-tuple-element.291, s32[]{:T(128)S(6)} %select_n.115), kind=kOutput, calls=%fused_computation.17.clone.1 | convolution fusion | flops 1090519040 | bytes 20201476 | tf_op jit(solution)/shard_map/while/body/eval_jaxpr/gmn,nd->mgd/dot_general | solution.py:97
  258.4 5.3 %fusion.62 = bf16[1024,4,128]{0,2,1:T(8,128)(2,1)S(1)} fusion(f32[128,4,1024]{2,0,1:T(8,128)} %fusion.60, f32[1024,1024,4]{1,0,2:T(8,128)S(1)} %get-tuple-element.250, f32[4,1024]{1,0:T(4,128)S(1)} %max.13, pred[1024,1024]{0,1:T(8,128)(4,1)S(1)} %get-tuple-element.247, f32[1024,4]{0,1:T(4,128)S(1)} %add_bitcast_fusion.2, ...), kind=kOutput, calls=%fused_computation.25.clone.1 | convolution fusion | flops 1092091904 | bytes 21266436 | tf_op jit(solution)/shard_map/while/body/eval_jaxpr/gmn,nd->mgd/dot_general | solution.py:91
  268.7 2.5 compare_and_fusion.3
  271.2 1.6 constant_dynamic-slice_fusion.11
  272.8 3.0 fusion.59
  275.9 8.5 %fusion.58 = (f32[4,1024]{1,0:T(4,128)S(1)}, f32[1024,1024,4]{1,0,2:T(8,128)}) fusion(pred[1024,1024]{0,1:T(8,128)(4,1)S(1)} %get-tuple-element.245, bf16[1,1024,1,4,128]{4,3,1,0,2:T(4,128)(2,1)S(1)} %constant_dynamic-slice_fusion.11, bf16[2,1,1024,128]{2,3,1,0:T(8,128)(2,1)} %get-tuple-element.290, s32[]{:T(128)S(6)} %select_n.115), kind=kOutput, calls=%fused_computation.5.clone.1 | convolution fusion | flops 1086320640 | bytes 19152900 | tf_op jit(solution)/shard_map/while/body/eval_jaxpr/mgd,nd->gmn/dot_general | solution.py:79
  284.4 9.9 %fusion.61 = (f32[4,1024]{1,0:T(4,128)S(1)}, f32[4,1024]{1,0:T(4,128)S(1)}) fusion(f32[1024,1024,4]{1,0,2:T(8,128)} %get-tuple-element.246, f32[4,1024]{1,0:T(4,128)S(1)} %max.13, pred[1024,1024]{0,1:T(8,128)(4,1)S(1)} %get-tuple-element.245, f32[1024,1024,4]{1,0,2:T(8,128)S(1)} %get-tuple-element.250, pred[1024,1024]{0,1:T(8,128)(4,1)S(1)} %get-tuple-element.247), kind=kLoop, calls=%fused_computation.15.clone.1 | loop fusion | flops 33546240 | bytes 35700736 | tf_op jit(solution)/shard_map/while/body/eval_jaxpr/reduce_sum | solution.py:90
  294.4 11.0 %fusion.60 = f32[128,4,1024]{2,0,1:T(8,128)} fusion(f32[1024,1024,4]{1,0,2:T(8,128)} %get-tuple-element.246, f32[4,1024]{1,0:T(4,128)S(1)} %max.13, pred[1024,1024]{0,1:T(8,128)(4,1)S(1)} %get-tuple-element.245, bf16[2,1,1024,128]{2,3,1,0:T(8,128)(2,1)} %get-tuple-element.291, s32[]{:T(128)S(6)} %select_n.115), kind=kOutput, calls=%fused_computation.17.clone.1 | convolution fusion | flops 1090519040 | bytes 20201476 | tf_op jit(solution)/shard_map/while/body/eval_jaxpr/gmn,nd->mgd/dot_general | solution.py:97
  305.4 5.3 %fusion.62 = bf16[1024,4,128]{0,2,1:T(8,128)(2,1)S(1)} fusion(f32[128,4,1024]{2,0,1:T(8,128)} %fusion.60, f32[1024,1024,4]{1,0,2:T(8,128)S(1)} %get-tuple-element.250, f32[4,1024]{1,0:T(4,128)S(1)} %max.13, pred[1024,1024]{0,1:T(8,128)(4,1)S(1)} %get-tuple-element.247, f32[1024,4]{0,1:T(4,128)S(1)} %add_bitcast_fusion.2, ...), kind=kOutput, calls=%fused_computation.25.clone.1 | convolution fusion | flops 1092091904 | bytes 21266436 | tf_op jit(solution)/shard_map/while/body/eval_jaxpr/gmn,nd->mgd/dot_general | solution.py:91
  312.3 31.6 %all_to_all.73 = bf16[8,256,512]{2,1,0:T(8,128)(2,1)S(1)} all-to-all(bf16[8,256,512]{2,1,0:T(8,128)(2,1)} %bitcast.160), channel_id=1, replica_groups=mesh['blk'=16,'uly'=8] {'uly'}, dimensions={0} | all-to-all | bytes 4194304 | tf_op jit(solution)/shard_map/all_to_all | solution.py:109
  343.9 2.4 copy.56
  346.3 4.1 %copy.57 = bf16[256,4096]{1,0:T(8,128)(2,1)} copy(bf16[256,4096]{0,1:T(8,128)(2,1)} %bitcast.158) | data formatting | bytes 4194304 | tf_op jit(solution)/shard_map/all_to_all | solution.py:109
  (52 shorter events, 10.9 us)
Async XLA Ops:
  6.5 7.7 %copy-start = (bf16[256,1024]{1,0:T(8,128)(2,1)S(1)}, bf16[256,1024]{1,0:T(8,128)(2,1)}, u32[]{:S(2)}) copy-start(bf16[256,1024]{1,0:T(8,128)(2,1)} %param.8) | copy-start | bytes 1572868
  6.5 32.6 %copy-start.2 = (bf16[256,4096]{1,0:T(8,128)(2,1)S(1)}, bf16[256,4096]{1,0:T(8,128)(2,1)}, u32[]{:S(2)}) copy-start(bf16[256,4096]{1,0:T(8,128)(2,1)} %param.7) | copy-start | bytes 6291460
  6.5 38.9 %copy-start.5 = (s32[4]{0:T(128)S(1)}, s32[4]{0:T(128)}, u32[]{:S(2)}) copy-start(s32[4]{0:T(128)} %param.10) | copy-start | bytes 52
  8.7 15.1 %all-to-all-start = ((bf16[256,8,128]{0,2,1:T(8,128)(2,1)}), bf16[256,8,128]{0,2,1:T(8,128)(2,1)S(1)}, u32[]{:S(2)}, u32[]{:S(2)}) async-start(bf16[256,8,128]{0,2,1:T(8,128)(2,1)} %bitcast.162), calls=%async_computation | async-start | bytes 1048576 | tf_op jit(solution)/shard_map/all_to_all | solution.py:34
  23.8 13.0 %all-to-all-start.1 = ((bf16[256,8,128]{2,0,1:T(8,128)(2,1)}), bf16[256,8,128]{2,0,1:T(8,128)(2,1)S(1)}, u32[]{:S(2)}, u32[]{:S(2)}) async-start(bf16[256,8,128]{2,0,1:T(8,128)(2,1)} %copy_bitcast_fusion.4), calls=%async_computation.1 | async-start | bytes 1048576 | tf_op jit(solution)/shard_map/all_to_all | solution.py:33
  27.3 133.2 %all-gather.2.cloned.1.call-start = ((), (), s32[]{:S(2)}) async-start(), calls=%async_computation.4 | async-start | bytes 17825792 | tf_op jit(solution)/shard_map/all_gather | solution.py:14
  36.8 8.6 %copy-start.3 = (bf16[256,8,128]{2,0,1:T(8,128)(2,1)}, bf16[256,8,128]{2,0,1:T(8,128)(2,1)S(1)}, u32[]{:S(2)}) copy-start(bf16[256,8,128]{2,0,1:T(8,128)(2,1)S(1)} %all-to-all-done.1) | copy-start | bytes 1572868
  40.7 39.5 %all-to-all-start.2 = ((bf16[256,8,512]{2,0,1:T(8,128)(2,1)}), bf16[256,8,512]{2,0,1:T(8,128)(2,1)S(1)}, u32[]{:S(2)}, u32[]{:S(2)}) async-start(bf16[256,8,512]{2,0,1:T(8,128)(2,1)} %bitcast.156), calls=%async_computation.2 | async-start | bytes 4194304 | tf_op jit(solution)/shard_map/all_to_all | solution.py:32
  171.8 46.6 %copy-start.4 = (bf16[256,8,128]{2,0,1:T(8,128)(2,1)S(1)}, bf16[256,8,128]{2,0,1:T(8,128)(2,1)}, u32[]{:S(2)}) copy-start(bf16[256,8,128]{2,0,1:T(8,128)(2,1)} %copy-done.3) | copy-start | bytes 1572868
  312.3 38.1 %copy-start.1 = (bf16[256,1024]{1,0:T(8,128)(2,1)S(1)}, bf16[256,1024]{1,0:T(8,128)(2,1)}, u32[]{:S(2)}) copy-start(bf16[256,1024]{1,0:T(8,128)(2,1)} %param.8) | copy-start | bytes 1572868
Sparse Core Ops, SparseCore 0:
  39.3 121.1 all-gather.1
